TPU v7x, 256 devices: a whole 4x4x8 slice. The times are simulated.
256 devices in a mesh: frame: 16 (over z_hi, y), space: 16 (over z_lo, x, core).
Axes of the slice: x: 4, y: 4, z: 8 (z_hi: 4, z_lo: 2; z = z_hi * 2 + z_lo), core: 2. Of those that a mesh axis runs over, the one named last changes fastest.
Arguments:
- hidden_in: bfloat16 [2, 16, 32, 64, 1152], P(None, 'frame', 'space'), may hold values from -6 to 6
- attn_cotangent: bfloat16 [2, 16, 32, 64, 1152], P(None, 'frame', 'space'), may hold values from -6 to 6
- w_qkv: bfloat16 [1152, 3456], P('space'), may hold values from -0.1875 to 0.1875
- modulation_table: bfloat16 [1000, 2, 1152], replicated, may hold values from -3 to 3
- snr_table: float32 [1000], replicated, may hold values from 0.1 to 1
- timestep: int32 [2], replicated, may hold values from 0 to 999
- weight_index: int32 [2], replicated, may hold values from 0 to 999
Outputs:
- grad_input: bfloat16 [2, 16, 32, 64, 1152], P(None, 'frame', 'space')
- grad_w_qkv: float32 [1152, 3456], P('space')
- grad_modulation: float32 [2, 2, 1152], replicated
All inputs are finite; a program needn't handle non-finite values.
Results may differ from a plain program's by a relative error of at most 0.029.
Values may be sent and summed in bfloat16 or wider, within the bound.
A program may use at most 128 MiB of HBM per device.

v0:
```python
import jax
import jax.numpy as jnp
from jax import lax
from jax.sharding import PartitionSpec as P

HEADS = 16
HEAD_DIM = 72


def attend_back(queries, keys, values, upstream):
    factor = queries.shape[-1] ** (-0.5)
    queries = queries.astype(jnp.float32)
    keys = keys.astype(jnp.float32)
    values = values.astype(jnp.float32)
    upstream = upstream.astype(jnp.float32)
    highest = lax.Precision.HIGHEST
    scores = jnp.einsum("bfxhe,bgxhe->bxhfg", queries, keys, precision=highest) * factor
    expd = jnp.exp(scores)
    probs = expd / jnp.sum(expd, axis=-1, keepdims=True)
    grad_probs = jnp.einsum("bfxhe,bgxhe->bxhfg", upstream, values, precision=highest)
    grad_values = jnp.einsum("bxhfg,bfxhe->bgxhe", probs, upstream, precision=highest)
    grad_scores = probs * (grad_probs - jnp.sum(probs * grad_probs, axis=-1, keepdims=True))
    grad_queries = jnp.einsum("bxhfg,bgxhe->bfxhe", grad_scores, keys, precision=highest) * factor
    grad_keys = jnp.einsum("bxhfg,bfxhe->bgxhe", grad_scores, queries, precision=highest) * factor
    return (
        grad_queries.astype(jnp.bfloat16),
        grad_keys.astype(jnp.bfloat16),
        grad_values.astype(jnp.bfloat16),
    )


def per_device(
    hidden_in, attn_cotangent, w_qkv, modulation_table, snr_table, timestep, weight_index
):
    clip_count, frame_dev, row_dev, col_count, model_width = hidden_in.shape
    positions = row_dev * col_count
    values_in = hidden_in.astype(jnp.float32)
    average = jnp.mean(values_in, axis=-1, keepdims=True)
    centered = values_in - average
    variance = jnp.mean(centered * centered, axis=-1, keepdims=True)
    inverse_std = lax.rsqrt(variance + 1e-06)
    normed = centered * inverse_std
    modulation = modulation_table[timestep].astype(jnp.float32)
    shift = modulation[:, 0][:, None, None, None, :]
    scale = modulation[:, 1][:, None, None, None, :]
    modulated = (normed * (1.0 + scale) + shift).astype(jnp.bfloat16)
    mod_rows = modulated.reshape(-1, model_width)
    w_full = lax.all_gather(w_qkv, "space", axis=0, tiled=True)
    projected = jnp.dot(mod_rows, w_full, preferred_element_type=jnp.float32).astype(jnp.bfloat16)
    projected = projected.reshape(clip_count, frame_dev, positions, 3, model_width)
    loss_weight = snr_table[weight_index]
    upstream = (loss_weight[:, None, None, None, None] * attn_cotangent.astype(jnp.float32)).astype(
        jnp.bfloat16
    )
    upstream = upstream.reshape(clip_count, frame_dev, positions, 1, model_width)
    packed = jnp.concatenate([projected, upstream], axis=3)
    received = lax.all_to_all(packed, "frame", split_axis=2, concat_axis=1, tiled=True)
    item_count = received.shape[0]
    frames = received.shape[1]
    across = received.shape[2]
    pieces = received.reshape(item_count, frames, across, 4, HEADS, HEAD_DIM)
    head_grads = attend_back(
        pieces[:, :, :, 0], pieces[:, :, :, 1], pieces[:, :, :, 2], pieces[:, :, :, 3]
    )
    stacked = jnp.stack(head_grads, axis=3).reshape(item_count, frames, across, 3, model_width)
    grad_projected = lax.all_to_all(stacked, "frame", split_axis=1, concat_axis=2, tiled=True)
    grad_rows = grad_projected.reshape(-1, 3 * model_width)
    device_count = lax.axis_size("frame") * lax.axis_size("space")
    grad_scale_factor = float(mod_rows.shape[0] * device_count) ** (-0.5)
    row_share = lax.psum_scatter(
        lax.dot_general(
            mod_rows, grad_rows, (((0,), (0,)), ((), ())), preferred_element_type=jnp.float32
        ).astype(jnp.bfloat16),
        "space",
        scatter_dimension=0,
        tiled=True,
    )
    grad_weight = lax.psum(row_share, "frame").astype(jnp.float32) * grad_scale_factor
    grad_hidden = lax.dot_general(
        grad_rows, w_full, (((1,), (1,)), ((), ())), preferred_element_type=jnp.float32
    )
    grad_hidden = grad_hidden.reshape(values_in.shape)
    local_sums = jnp.stack(
        [jnp.sum(grad_hidden, axis=(1, 2, 3)), jnp.sum(grad_hidden * normed, axis=(1, 2, 3))],
        axis=1,
    )
    grad_modulation = lax.psum(local_sums, ("frame", "space")) * grad_scale_factor
    grad_normed = grad_hidden * (1.0 + scale)
    grad_input = (
        grad_normed
        - jnp.mean(grad_normed, axis=-1, keepdims=True)
        - normed * jnp.mean(grad_normed * normed, axis=-1, keepdims=True)
    ) * inverse_std
    return (grad_input.astype(jnp.bfloat16), grad_weight, grad_modulation)


def solution(mesh):
    in_specs = (
        P(None, "frame", "space", None, None),
        P(None, "frame", "space", None, None),
        P("space", None),
        P(),
        P(),
        P(),
        P(),
    )
    out_specs = (P(None, "frame", "space", None, None), P("space", None), P())
    return jax.shard_map(
        per_device, mesh=mesh, in_specs=in_specs, out_specs=out_specs, check_vma=False
    )
```

profile of v0, /device:TPU:2, one launch (start us, length us, event | category | flops | bytes accessed | tf_op | source)
XLA Modules:
  0.0 491.3 jit_solution(7075564899825200032)
XLA Ops:
  7.2 0.7 all-gather.2.cloned.1.call-update
  8.6 2.9 gather_fusion
  11.6 0.7 compare_select_fusion
  12.9 1.2 multiply_convert_fusion.2
  15.6 49.8 %all-gather.2.cloned.1.call-done = bf16[1152,3456]{1,0:T(8,128)(2,1)} async-done(((bf16[72,3456]{1,0:T(8,128)(2,1)}), bf16[1152,3456]{1,0:T(8,128)(2,1)}) %all-gather.2.cloned.1.call-update) | async-done | bytes 7962640 | tf_op jit(solution)/shard_map/all_gather | solution.py:48
  65.5 7.1 %convolution_convert_fusion.1 = bf16[256,3456]{1,0:T(8,128)(2,1)} fusion(bf16[256,1152]{1,0:T(8,128)(2,1)S(1)} %bitcast.76, bf16[1152,3456]{1,0:T(8,128)(2,1)} %all-gather.2.cloned.1.call-done), kind=kOutput, calls=%fused_computation.3 | convolution fusion | flops 2039316480 | bytes 10321920 | tf_op jit(solution)/shard_map/dot_general | solution.py:49
  72.6 2.6 copy.63
  75.2 2.0 reshape.124
  77.2 4.6 pad_maximum_fusion
  81.8 4.9 copy.66
  86.7 67.7 %all_to_all.8 = bf16[2,1,128,4,1152]{4,3,1,0,2:T(4,128)(2,1)S(1)} all-to-all(bf16[2,1,128,4,1152]{4,3,1,0,2:T(4,128)(2,1)} %copy.66), channel_id=1, replica_groups=mesh['frame'=16,'space'=16] {'frame'}, dimensions={2} | all-to-all | bytes 4718592 | tf_op jit(solution)/shard_map/all_to_all | solution.py:57
  154.4 8.8 %reshape.148 = bf16[2,16,8,4,16,72]{5,4,3,0,2,1:T(8,128)(2,1)} reshape(bf16[2,1,128,4,1152]{4,3,1,0,2:T(4,128)(2,1)S(1)} %all_to_all.8) | data formatting | bytes 4718592 | tf_op jit(solution)/shard_map/reshape | solution.py:61
  163.2 3.6 fusion.25
  166.8 1.7 fusion.1
  168.5 1.8 multiply_reduce_fusion
  170.2 2.4 fusion.9
  172.7 2.2 fusion.10
  174.9 3.0 fusion.8
  178.2 1.5 stack.21
  180.0 1.3 stack.22
  181.4 1.5 copy.75
  182.9 1.3 stack.23
  184.6 40.6 %all_to_all.9 = bf16[2,16,8,3,1152]{4,2,0,3,1:T(8,128)(2,1)S(1)} all-to-all(bf16[2,16,8,3,1152]{4,2,0,3,1:T(8,128)(2,1)S(1)} %copy.76), channel_id=1, replica_groups=mesh['frame'=16,'space'=16] {'frame'}, dimensions={1} | all-to-all | bytes 3538944 | tf_op jit(solution)/shard_map/all_to_all | solution.py:66
  225.2 0.9 copy.77
  226.4 0.8 copy-done.4
  227.2 5.5 %convolution_convert_fusion = bf16[1152,3456]{1,0:T(8,128)(2,1)} fusion(bf16[256,1152]{1,0:T(8,128)(2,1)S(1)} %bitcast.77, bf16[256,3456]{1,0:T(8,128)(2,1)S(1)} %bitcast.73), kind=kOutput, calls=%fused_computation.2 | convolution fusion | flops 2042413056 | bytes 10321920 | tf_op jit(solution)/shard_map/dot_general | solution.py:71
  232.8 6.5 %fusion.19 = (f32[256]{0:T(256)}, f32[256,1152]{1,0:T(8,128)S(1)}) fusion(f32[2,1152]{1,0:T(2,128)S(1)} %bitcast.80, bf16[256,3456]{1,0:T(8,128)(2,1)S(1)} %bitcast.74, bf16[1152,3456]{1,0:T(8,128)(2,1)} %all-gather.2.cloned.1.call-done), kind=kOutput, calls=%fused_computation.34 | convolution fusion | flops 2039021312 | bytes 10921984 | tf_op jit(solution)/shard_map/dot_general | solution.py:79
  239.4 1.2 fusion.17
  240.6 77.9 %psum.15 = f32[2,2,1152]{2,0,1:T(2,128)S(1)} all-reduce(f32[2,2,1152]{2,0,1:T(2,128)S(1)} %pad_maximum_fusion.2), channel_id=1, replica_groups=mesh['frame'=16,'space'=16] {'frame','space'}, use_global_device_ids=true, to_apply=%region_10.0 | all-reduce | flops 4608 | bytes 36864 | tf_op jit(solution)/shard_map/psum | solution.py:87
  319.3 1.9 fusion.16
  321.2 161.5 %all-reduce.3.cloned.1.call-done = bf16[72,3456]{1,0:T(8,128)(2,1)} async-done(((bf16[72,3456]{1,0:T(8,128)(2,1)}), bf16[72,3456]{1,0:T(8,128)(2,1)}) %all-reduce.3.cloned.1.call-update) | async-done | bytes 497680 | tf_op jit(solution)/shard_map/psum | solution.py:78
  482.7 2.0 convert_multiply_fusion
  (50 shorter events, 4.9 us)
Async XLA Ops:
  7.2 5.1 %copy-start = (f32[1000]{0:T(1024)S(1)}, f32[1000]{0:T(1024)}, u32[]{:S(2)}) copy-start(f32[1000]{0:T(1024)} %param.11) | copy-start | bytes 12004
  7.2 7.6 %copy-start.2 = (bf16[2,1,2,64,1152]{4,3,2,1,0:T(8,128)(2,1)S(1)}, bf16[2,1,2,64,1152]{4,3,2,1,0:T(8,128)(2,1)}, u32[]{:S(2)}) copy-start(bf16[2,1,2,64,1152]{4,3,2,1,0:T(8,128)(2,1)} %param.7) | copy-start | bytes 1769476
  7.2 58.3 %all-gather.2.cloned.1.call-start = ((), (), s32[]{:S(2)}) async-start(), calls=%async_computation.3 | async-start | bytes 8460288 | tf_op jit(solution)/shard_map/all_gather | solution.py:48
  7.9 311.4 %reduce-scatter.5.cloned.1.call-start = ((), (), s32[]{:S(2)}) async-start(), calls=%async_computation.5 | async-start | bytes 8460288
  15.0 224.4 %copy-start.5 = (f32[2,2,64]{2,1,0:T(2,128)}, f32[2,2,64]{2,1,0:T(2,128)S(1)}, u32[]{:S(2)}) copy-start(f32[2,2,64]{2,1,0:T(2,128)S(1)} %broadcast_multiply_fusion.2) | copy-start | bytes 3076
  15.3 50.2 %copy-start.6 = (f32[2,2,64]{2,1,0:T(2,128)}, f32[2,2,64]{2,1,0:T(2,128)S(1)}, u32[]{:S(2)}) copy-start(f32[2,2,64]{2,1,0:T(2,128)S(1)} %add_rsqrt_fusion) | copy-start | bytes 3076
  15.6 49.8 %copy-start.3 = (bf16[2,1,2,64,1152]{4,3,2,1,0:T(8,128)(2,1)}, bf16[2,1,2,64,1152]{4,3,2,1,0:T(8,128)(2,1)S(1)}, u32[]{:S(2)}) copy-start(bf16[2,1,2,64,1152]{4,3,2,1,0:T(8,128)(2,1)S(1)} %fusion.12) | copy-start | bytes 1769476
  226.1 1.1 copy-start.4
  232.7 250.0 %all-reduce.3.cloned.1.call-start = ((), (), s32[]{:S(2)}) async-start(), calls=%async_computation.4 | async-start | bytes 995328 | tf_op jit(solution)/shard_map/psum | solution.py:78
  239.3 79.9 %copy-start.8 = (f32[256]{0:T(256)S(1)}, f32[256]{0:T(256)}, u32[]{:S(2)}) copy-start(f32[256]{0:T(256)} %get-tuple-element.25) | copy-start | bytes 3076
  239.4 79.9 %copy-start.7 = (f32[2,2,64]{2,1,0:T(2,128)S(1)}, f32[2,2,64]{2,1,0:T(2,128)}, u32[]{:S(2)}) copy-start(f32[2,2,64]{2,1,0:T(2,128)} %copy-done.6) | copy-start | bytes 3076
  319.3 165.5 %copy-start.1 = (f32[1000]{0:T(1024)S(1)}, f32[1000]{0:T(1024)}, u32[]{:S(2)}) copy-start(f32[1000]{0:T(1024)} %param.11) | copy-start | bytes 12004
Sparse Core Ops, SparseCore 0:
  9.9 55.5 all-gather.1
  232.9 74.6 reduce-scatter.4
  319.4 163.2 all-reduce.2
where the time goes:
time: 492 us; the launch traced here: 491 us
  waiting for transfers between devices  212 us (43%)
  blocking collectives  186 us (38%)
  local copies, waits for them, and re-layouts  35.1 us (7%)
  matrix products  30.3 us (6%)
  between operations  14 us (3%)
  other arithmetic  13.4 us (3%)
    psum x1, waiting for transfers between devices, per_device(): lax.psum(row_share, 'frame').astype(jnp.float32) * grad_scale_factor  162 us
    psum x1, blocking collectives, per_device(): lax.psum(local_sums, ('frame', 'space')) * grad_scale_factor  77.9 us
    all_to_all x1, blocking collectives, per_device(): lax.all_to_all(packed, 'frame', split_axis=2, concat_axis=1, tiled=True)  67.7 us
    all_gather x1, waiting for transfers between devices, per_device(): w_full = lax.all_gather(w_qkv, 'space', axis=0, tiled=True)  49.8 us
    all_to_all x1, blocking collectives, per_device(): lax.all_to_all(stacked, 'frame', split_axis=1, concat_axis=2, tiled=True)  40.6 us
  transfers between devices with their start and end apart: 3, of which 2 were waited for; matrix products, arithmetic and copies ran while one was open for 4% of the time, Pallas kernels for 0%

commit v1 on v0

--- a/solution.py
+++ b/solution.py
@@ -54,7 +54,10 @@
     )
     upstream = upstream.reshape(clip_count, frame_dev, positions, 1, model_width)
     packed = jnp.concatenate([projected, upstream], axis=3)
-    received = lax.all_to_all(packed, "frame", split_axis=2, concat_axis=1, tiled=True)
+    received = jnp.concatenate(
+        lax.all_to_all(jnp.stack(jnp.split(packed, lax.axis_size("frame"), axis=2)), "frame", 0, 0),
+        axis=1,
+    )
     item_count = received.shape[0]
     frames = received.shape[1]
     across = received.shape[2]

time: 492 us -> 668 us (1.36); the launches traced: 491 us -> 657 us
  local copies, waits for them, and re-layouts: 35.1 us -> 127 us
  other arithmetic: 13.4 us -> 87.7 us
    another operation x0 -> x18, local copies, waits for them, and re-layouts: none -> 96.4 us  [the longest x17 88 us: per_device(): jnp.stack(jnp.split(packed, lax.axis_size('frame'), axis=2))]
    another operation x0 -> x4, other arithmetic: none -> 79.6 us  [per_device(): jnp.stack(jnp.split(packed, lax.axis_size('frame'), axis=2))]
    reshape x1 -> x0, local copies, waits for them, and re-layouts: 8.77 us -> none  [per_device(): pieces = received.reshape(item_count, frames, across, 4, HEADS, HEAD_DIM)]
    unnamed x22 -> x55, local copies, waits for them, and re-layouts: 1.72 us -> 9.38 us
  transfers between devices with their start and end apart: 3 -> 3, of which waited for: 2 -> 2; matrix products, arithmetic and copies ran while one was open for 4% -> 3% of each run, Pallas kernels for 0% -> 0%
where the time goes in v1:
time: 668 us; the launch traced here: 657 us
  waiting for transfers between devices  212 us (32%)
  blocking collectives  188 us (28%)
  local copies, waits for them, and re-layouts  127 us (19%)
  other arithmetic  87.7 us (13%)
  matrix products  28.4 us (4%)
  between operations  14.6 us (2%)
    psum x1, waiting for transfers between devices, per_device(): lax.psum(row_share, 'frame').astype(jnp.float32) * grad_scale_factor  162 us
    another operation x17, local copies, waits for them, and re-layouts, per_device(): jnp.stack(jnp.split(packed, lax.axis_size('frame'), axis=2))  88 us
    another operation x4, other arithmetic, per_device(): jnp.stack(jnp.split(packed, lax.axis_size('frame'), axis=2))  79.6 us
    psum x1, blocking collectives, per_device(): lax.psum(local_sums, ('frame', 'space')) * grad_scale_factor  79.4 us
    all_to_all x1, blocking collectives, per_device(): lax.all_to_all(jnp.stack(jnp.split(packed, lax.axis_size('frame'), axis=2...  67.5 us
    all_gather x1, waiting for transfers between devices, per_device(): w_full = lax.all_gather(w_qkv, 'space', axis=0, tiled=True)  49.8 us
    all_to_all x1, blocking collectives, per_device(): lax.all_to_all(stacked, 'frame', split_axis=1, concat_axis=2, tiled=True)  40.6 us
  transfers between devices with their start and end apart: 3, of which 2 were waited for; matrix products, arithmetic and copies ran while one was open for 3% of the time, Pallas kernels for 0%

profile of v1, /device:TPU:2, one launch (start us, length us, event | category | flops | bytes accessed | tf_op | source)
XLA Modules:
  0.0 657.4 jit_solution(16833431120377244466)
XLA Ops:
  9.3 2.9 gather_fusion
  15.6 49.8 %all-gather.2.cloned.1.call-done = bf16[1152,3456]{1,0:T(8,128)(2,1)} async-done(((bf16[72,3456]{1,0:T(8,128)(2,1)}), bf16[1152,3456]{1,0:T(8,128)(2,1)}) %all-gather.2.cloned.1.call-update) | async-done | bytes 7962640 | tf_op jit(solution)/shard_map/all_gather | solution.py:48
  65.4 5.8 convolution_convert_fusion.1
  73.6 3.6 reshape.120
  77.2 15.6 %maximum_bitcast_fusion.2 = (bf16[1,2,1,8,4,1152]{3,1,5,4,2,0:T(2,128)(2,1)}, bf16[1,2,1,8,4,1152]{3,1,5,4,2,0:T(2,128)(2,1)}, bf16[1,2,1,8,4,1152]{3,1,5,4,2,0:T(2,128)(2,1)}) fusion(bf16[2,1,128,1,1152]{2,0,4,3,1:T(2,128)(2,1)S(1)} %copy.47, bf16[2,1,128,3,1152]{2,0,4,3,1:T(2,128)(2,1)S(1)} %reshape.120), kind=kLoop, calls=%fused_computation.8 | loop fusion | flops 221184 | bytes 2801664 | tf_op jit(solution)/shard_map/stack | solution.py:58
  92.7 21.2 %maximum_bitcast_fusion.1 = (bf16[1,2,1,8,4,1152]{3,1,5,4,2,0:T(2,128)(2,1)}, bf16[1,2,1,8,4,1152]{3,1,5,4,2,0:T(2,128)(2,1)}, bf16[1,2,1,8,4,1152]{3,1,5,4,2,0:T(2,128)(2,1)}, bf16[1,2,1,8,4,1152]{3,1,5,4,2,0:T(2,128)(2,1)}) fusion(bf16[2,1,128,1,1152]{2,0,4,3,1:T(2,128)(2,1)S(1)} %copy.47, bf16[2,1,128,3,1152]{2,0,4,3,1:T(2,128)(2,1)S(1)} %reshape.120), kind=kLoop, calls=%fused_computation.7 | loop fusion | flops 294912 | bytes 2949120 | tf_op jit(solution)/shard_map/stack | solution.py:58
  114.0 21.2 %maximum_bitcast_fusion = (bf16[1,2,1,8,4,1152]{3,1,5,4,2,0:T(2,128)(2,1)}, bf16[1,2,1,8,4,1152]{3,1,5,4,2,0:T(2,128)(2,1)}, bf16[1,2,1,8,4,1152]{3,1,5,4,2,0:T(2,128)(2,1)}, bf16[1,2,1,8,4,1152]{3,1,5,4,2,0:T(2,128)(2,1)}) fusion(bf16[2,1,128,1,1152]{2,0,4,3,1:T(2,128)(2,1)S(1)} %copy.47, bf16[2,1,128,3,1152]{2,0,4,3,1:T(2,128)(2,1)S(1)} %reshape.120), kind=kLoop, calls=%fused_computation.6 | loop fusion | flops 294912 | bytes 2949120 | tf_op jit(solution)/shard_map/stack | solution.py:58
  135.2 21.5 %fusion = (bf16[1,2,1,8,4,1152]{3,1,5,4,2,0:T(2,128)(2,1)}, bf16[1,2,1,8,4,1152]{3,1,5,4,2,0:T(2,128)(2,1)}, bf16[1,2,1,8,4,1152]{3,1,5,4,2,0:T(2,128)(2,1)}, bf...) fusion(bf16[2,1,128,1,1152]{2,0,4,3,1:T(2,128)(2,1)S(1)} %copy.47, ...), kind=kLoop, calls=%fused_computation.5 | loop fusion | flops 1474560 | bytes 3096576 | tf_op jit(solution)/shard_map/stack | solution.py:58
  156.8 4.8 copy.60
  161.5 4.9 copy.58
  166.5 4.8 copy.59
  173.3 6.0 copy.55
  179.2 5.8 copy.56
  185.1 3.8 copy.57
  188.8 5.9 copy.62
  194.8 5.8 copy.52
  200.6 3.7 copy.53
  204.3 6.0 copy.54
  210.3 5.8 copy.63
  216.1 3.8 copy.48
  219.8 6.0 copy.49
  225.8 5.8 copy.50
  231.6 13.3 %copy.51 = bf16[1,2,1,8,4,1152]{5,3,4,2,1,0:T(8,128)(2,1)} copy(bf16[1,2,1,8,4,1152]{3,1,5,4,2,0:T(2,128)(2,1)S(1)} %copy-done.3) | data formatting | bytes 294912 | tf_op jit(solution)/shard_map/stack | solution.py:58
  252.7 67.5 %all_to_all.14 = bf16[16,2,1,8,4,1152]{5,3,4,2,1,0:T(8,128)(2,1)S(1)} all-to-all(bf16[16,2,1,8,4,1152]{5,3,4,2,1,0:T(8,128)(2,1)S(1)} %constant_dynamic-update-slice_fusion), channel_id=1, replica_groups=mesh['frame'=16,'space'=16] {'frame'}, dimensions={0} | all-to-all | bytes 4718592 | tf_op jit(solution)/shard_map/all_to_all | solution.py:58
  320.2 8.3 %reshape.144 = bf16[2,16,8,4,16,72]{5,4,2,3,0,1:T(8,128)(2,1)} reshape(bf16[2,16,1,8,4,1152]{5,3,4,2,0,1:T(8,128)(2,1)S(1)} %bitcast.110) | data formatting | bytes 4718592 | tf_op jit(solution)/shard_map/reshape;reshape | solution.py:64
  328.5 3.8 fusion.26
  337.7 3.3 fusion.11
  350.0 40.6 %all_to_all.15 = bf16[2,16,8,3,1152]{4,2,0,3,1:T(8,128)(2,1)S(1)} all-to-all(bf16[2,16,8,3,1152]{4,2,0,3,1:T(8,128)(2,1)S(1)} %copy.73), channel_id=1, replica_groups=mesh['frame'=16,'space'=16] {'frame'}, dimensions={1} | all-to-all | bytes 3538944 | tf_op jit(solution)/shard_map/all_to_all | solution.py:69
  392.6 5.5 convolution_convert_fusion
  398.2 5.9 fusion.20
  405.5 79.4 %psum.15 = f32[2,2,1152]{2,0,1:T(2,128)S(1)} all-reduce(f32[2,2,1152]{2,0,1:T(2,128)S(1)} %pad_maximum_fusion.2), channel_id=1, replica_groups=mesh['frame'=16,'space'=16] {'frame','space'}, use_global_device_ids=true, to_apply=%region_10.0 | all-reduce | flops 4608 | bytes 36864 | tf_op jit(solution)/shard_map/psum | solution.py:90
  486.9 161.5 %all-reduce.3.cloned.1.call-done = bf16[72,3456]{1,0:T(8,128)(2,1)} async-done(((bf16[72,3456]{1,0:T(8,128)(2,1)}), bf16[72,3456]{1,0:T(8,128)(2,1)}) %all-reduce.3.cloned.1.call-update) | async-done | bytes 497680 | tf_op jit(solution)/shard_map/psum | solution.py:81
  (101 shorter events, 39.2 us)
Async XLA Ops:
  7.2 5.1 copy-start
  7.2 7.6 %copy-start.2 = (bf16[2,1,2,64,1152]{4,3,2,1,0:T(8,128)(2,1)S(1)}, bf16[2,1,2,64,1152]{4,3,2,1,0:T(8,128)(2,1)}, u32[]{:S(2)}) copy-start(bf16[2,1,2,64,1152]{4,3,2,1,0:T(8,128)(2,1)} %param.7) | copy-start | bytes 1769476
  7.2 58.2 %all-gather.2.cloned.1.call-start = ((), (), s32[]{:S(2)}) async-start(), calls=%async_computation.3 | async-start | bytes 8460288 | tf_op jit(solution)/shard_map/all_gather | solution.py:48
  7.9 477.7 %reduce-scatter.5.cloned.1.call-start = ((), (), s32[]{:S(2)}) async-start(), calls=%async_computation.5 | async-start | bytes 8460288
  15.0 56.3 %copy-start.14 = (f32[2,2,64]{2,1,0:T(2,128)}, f32[2,2,64]{2,1,0:T(2,128)S(1)}, u32[]{:S(2)}) copy-start(f32[2,2,64]{2,1,0:T(2,128)S(1)} %broadcast_multiply_fusion.2) | copy-start | bytes 3076
  15.3 50.1 %copy-start.16 = (f32[2,2,64]{2,1,0:T(2,128)}, f32[2,2,64]{2,1,0:T(2,128)S(1)}, u32[]{:S(2)}) copy-start(f32[2,2,64]{2,1,0:T(2,128)S(1)} %add_rsqrt_fusion) | copy-start | bytes 3076
  15.6 55.7 %copy-start.8 = (bf16[2,1,2,64,1152]{4,3,2,1,0:T(8,128)(2,1)}, bf16[2,1,2,64,1152]{4,3,2,1,0:T(8,128)(2,1)S(1)}, u32[]{:S(2)}) copy-start(bf16[2,1,2,64,1152]{4,3,2,1,0:T(8,128)(2,1)S(1)} %fusion.13) | copy-start | bytes 1769476
  161.5 9.7 %copy-start.7 = (bf16[1,2,1,8,4,1152]{3,1,5,4,2,0:T(2,128)(2,1)S(1)}, bf16[1,2,1,8,4,1152]{3,1,5,4,2,0:T(2,128)(2,1)}, u32[]{:S(2)}) copy-start(bf16[1,2,1,8,4,1152]{3,1,5,4,2,0:T(2,128)(2,1)} %get-tuple-element.27) | copy-start | bytes 442372
  173.3 11.8 %copy-start.6 = (bf16[1,2,1,8,4,1152]{3,1,5,4,2,0:T(2,128)(2,1)S(1)}, bf16[1,2,1,8,4,1152]{3,1,5,4,2,0:T(2,128)(2,1)}, u32[]{:S(2)}) copy-start(bf16[1,2,1,8,4,1152]{3,1,5,4,2,0:T(2,128)(2,1)} %get-tuple-element.30) | copy-start | bytes 442372
  188.8 11.7 %copy-start.5 = (bf16[1,2,1,8,4,1152]{3,1,5,4,2,0:T(2,128)(2,1)S(1)}, bf16[1,2,1,8,4,1152]{3,1,5,4,2,0:T(2,128)(2,1)}, u32[]{:S(2)}) copy-start(bf16[1,2,1,8,4,1152]{3,1,5,4,2,0:T(2,128)(2,1)} %get-tuple-element.25) | copy-start | bytes 442372
  204.3 11.8 %copy-start.4 = (bf16[1,2,1,8,4,1152]{3,1,5,4,2,0:T(2,128)(2,1)S(1)}, bf16[1,2,1,8,4,1152]{3,1,5,4,2,0:T(2,128)(2,1)}, u32[]{:S(2)}) copy-start(bf16[1,2,1,8,4,1152]{3,1,5,4,2,0:T(2,128)(2,1)} %get-tuple-element.19) | copy-start | bytes 442372
  219.8 11.8 %copy-start.3 = (bf16[1,2,1,8,4,1152]{3,1,5,4,2,0:T(2,128)(2,1)S(1)}, bf16[1,2,1,8,4,1152]{3,1,5,4,2,0:T(2,128)(2,1)}, u32[]{:S(2)}) copy-start(bf16[1,2,1,8,4,1152]{3,1,5,4,2,0:T(2,128)(2,1)} %get-tuple-element.22) | copy-start | bytes 442372
  244.9 7.5 %copy-start.12 = (bf16[1,2,1,8,4,1152]{5,3,4,2,1,0:T(8,128)(2,1)S(1)}, bf16[1,2,1,8,4,1152]{5,3,4,2,1,0:T(8,128)(2,1)}, u32[]{:S(2)}) copy-start(bf16[1,2,1,8,4,1152]{5,3,4,2,1,0:T(8,128)(2,1)} %copy.56) | copy-start | bytes 442372
  244.9 7.6 %copy-start.13 = (bf16[1,2,1,8,4,1152]{5,3,4,2,1,0:T(8,128)(2,1)S(1)}, bf16[1,2,1,8,4,1152]{5,3,4,2,1,0:T(8,128)(2,1)}, u32[]{:S(2)}) copy-start(bf16[1,2,1,8,4,1152]{5,3,4,2,1,0:T(8,128)(2,1)} %copy.57) | copy-start | bytes 442372
  244.9 7.7 %copy-start.10 = (bf16[1,2,1,8,4,1152]{5,3,4,2,1,0:T(8,128)(2,1)S(1)}, bf16[1,2,1,8,4,1152]{5,3,4,2,1,0:T(8,128)(2,1)}, u32[]{:S(2)}) copy-start(bf16[1,2,1,8,4,1152]{5,3,4,2,1,0:T(8,128)(2,1)} %copy.62) | copy-start | bytes 442372
  244.9 7.7 %copy-start.11 = (bf16[1,2,1,8,4,1152]{5,3,4,2,1,0:T(8,128)(2,1)S(1)}, bf16[1,2,1,8,4,1152]{5,3,4,2,1,0:T(8,128)(2,1)}, u32[]{:S(2)}) copy-start(bf16[1,2,1,8,4,1152]{5,3,4,2,1,0:T(8,128)(2,1)} %copy.63) | copy-start | bytes 442372
  391.6 1.1 copy-start.9
  398.2 250.2 %all-reduce.3.cloned.1.call-start = ((), (), s32[]{:S(2)}) async-start(), calls=%async_computation.4 | async-start | bytes 995328 | tf_op jit(solution)/shard_map/psum | solution.py:81
  404.3 81.3 %copy-start.15 = (f32[2,2,64]{2,1,0:T(2,128)S(1)}, f32[2,2,64]{2,1,0:T(2,128)}, u32[]{:S(2)}) copy-start(f32[2,2,64]{2,1,0:T(2,128)} %copy-done.14) | copy-start | bytes 3076
  404.3 81.3 %copy-start.17 = (f32[2,2,64]{2,1,0:T(2,128)S(1)}, f32[2,2,64]{2,1,0:T(2,128)}, u32[]{:S(2)}) copy-start(f32[2,2,64]{2,1,0:T(2,128)} %copy-done.16) | copy-start | bytes 3076
  404.4 246.1 %copy-start.1 = (f32[1000]{0:T(1024)S(1)}, f32[1000]{0:T(1024)}, u32[]{:S(2)}) copy-start(f32[1000]{0:T(1024)} %param.11) | copy-start | bytes 12004
Sparse Core Ops, SparseCore 0:
  9.9 55.5 all-gather.1
  398.3 74.6 reduce-scatter.4
  485.7 162.6 all-reduce.2
